TPU v7x, 512 devices: a whole 4x4x16 slice. The times are simulated.
512 devices in a mesh: feeder: 32 (over x, y, core), scen: 16 (over z).
Axes of the slice: x: 4, y: 4, z: 16, core: 2. Of those that a mesh axis runs over, the one named last changes fastest.
Arguments:
- anchor: bfloat16 [256, 24, 16384], P('scen', None, 'feeder'), may hold values from -6 to 6
- cost_lin: bfloat16 [256, 24, 16384], P('scen', None, 'feeder'), may hold values from -6 to 6
- dual: float32 [256, 24, 16384], P('scen', None, 'feeder'), may hold values from -4 to 4
- target: float32 [256, 24], P('scen'), may hold values from -4 to 4
- leaf_weight: float32 [256], P('scen'), may hold values from 1 to 10
- q_mat: bfloat16 [16384, 512], P('feeder'), may hold values from -0.25 to 0.25
- diag_gain: float32 [16384], P('feeder'), may hold values from 0.5 to 2
- block_mask: int32 [32, 4, 4], P('feeder'), may hold values from 0 to 1, as said below
- ancestor: int32 [24, 256], P(None, 'scen'), may hold values from 0 to 255, as said below
Outputs:
- setpoints: float32 [256, 24, 16384], P('scen', None, 'feeder')
- average: float32 [256, 24, 16384], P('scen', None, 'feeder')
- new_dual: float32 [256, 24, 16384], P('scen', None, 'feeder')
Inputs may be any that keep to these rules, and one draw needn't show every extreme that they name: `block_mask`: every diagonal block is present; the share of present off-diagonal blocks differs from feeder to feeder. ancestor[t, s] is the first leaf of the section-t tree node that holds leaf s: the leaves of a node are consecutive, ancestor[0, s] = 0, and every section-t node lies inside one section-(t-1) node. Nodes may span several groups at any section.
All inputs are finite; a program needn't handle non-finite values.
Results may differ from a plain program's by a relative error of at most 0.0003.
Values sent between devices are 32-bit elements; how exact they have to be, the bound alone decides.
No kernel may reach another device: no remote copies, remote signals or barrier semaphores. Data moves between devices by JAX's collectives and lax.ppermute only.
A program may use at most 64 MiB of HBM per device.

v0:
```python
import jax
import jax.numpy as jnp
from jax import lax
from jax.sharding import PartitionSpec as P

PROX_ITERS = 8
penalty = 1.0
step_size = 0.08
coupling = 4.0
power_limit = 2.0


def link_terms(earlier, later):
    return (
        later[0] + later[2][:, None] * earlier[0],
        later[1] + later[2] * earlier[1],
        earlier[2] * later[2],
    )


def local(anchor, cost_lin, dual, target, leaf_weight, q_mat, diag_gain, block_mask, ancestor):
    leaves, sections, nodes = anchor.shape
    rows = leaves * sections
    count = block_mask.shape[1]
    width = nodes // count
    total_nodes = lax.axis_size("feeder") * nodes
    start_pt = anchor.astype(jnp.float32)
    fixed_part = cost_lin.astype(jnp.float32) + dual - penalty * start_pt
    diag_term = 2.0 * diag_gain + penalty
    expand = jnp.repeat(jnp.repeat(block_mask[0], width, axis=0), width, axis=1).astype(
        jnp.bfloat16
    )
    q_eff = q_mat * expand
    state = start_pt
    for sweep in range(PROX_ITERS):
        flat = state.reshape(rows, nodes).astype(jnp.bfloat16)
        image = jnp.dot(flat, q_eff, preferred_element_type=jnp.float32)
        head = lax.psum(jnp.sum(state, axis=2), "feeder") / total_nodes
        grad = image.reshape(leaves, sections, nodes) + diag_term * state + fixed_part
        grad = grad + coupling * (head - target)[:, :, None]
        state = jnp.clip(state - step_size * grad, -power_limit, power_limit)
    highest = lax.Precision.HIGHEST
    weighted = leaf_weight[:, None, None] * state
    first_leaf = lax.axis_index("scen") * leaves
    local_id = jnp.maximum(ancestor - first_leaf, 0)
    slot_ids = jnp.arange(leaves, dtype=jnp.int32)
    member = (local_id[:, None, :] == slot_ids[None, :, None]).astype(jnp.float32)
    seg_sums = jnp.einsum("tgl,ltn->tgn", member, weighted, precision=highest)
    seg_weights = jnp.einsum("tgl,l->tg", member, leaf_weight, precision=highest)
    last_pick = (slot_ids[None, :] == local_id[:, leaves - 1][:, None]).astype(jnp.float32)
    first_pick = (slot_ids[None, :] == 0).astype(jnp.float32)
    tail_sum = jnp.einsum("tg,tgn->tn", last_pick, seg_sums, precision=highest)
    tail_weight = jnp.sum(last_pick * seg_weights, axis=1)
    continued = (ancestor[:, 0] < first_leaf).astype(jnp.float32)
    spanning = (ancestor[:, leaves - 1] < first_leaf).astype(jnp.float32)
    head_sum = seg_sums[:, 0, :] * continued[:, None]
    head_weight = seg_weights[:, 0] * continued
    gathered = (
        lax.all_gather(tail_sum[None], "scen", axis=0, tiled=True),
        lax.all_gather(tail_weight[None], "scen", axis=0, tiled=True),
        lax.all_gather(head_sum[None], "scen", axis=0, tiled=True),
        lax.all_gather(head_weight[None], "scen", axis=0, tiled=True),
        lax.all_gather(spanning[None], "scen", axis=0, tiled=True),
    )
    position = lax.axis_index("scen")
    group_ids = jnp.arange(gathered[0].shape[0], dtype=jnp.int32)
    blank = (jnp.zeros_like(tail_sum), jnp.zeros_like(tail_weight), jnp.ones_like(spanning))

    def forward_step(carry, item):
        group, part_sum, part_weight, part_flag = item
        joined = link_terms(carry, (part_sum, part_weight, part_flag))
        keep = group < position
        return (
            jax.tree.map(lambda new_val, old_val: jnp.where(keep, new_val, old_val), joined, carry),
            None,
        )

    def backward_step(carry, item):
        group, part_sum, part_weight, part_flag = item
        joined = link_terms(carry, (part_sum, part_weight, part_flag))
        keep = group > position
        return (
            jax.tree.map(lambda new_val, old_val: jnp.where(keep, new_val, old_val), joined, carry),
            None,
        )

    before, unused = lax.scan(
        forward_step, blank, (group_ids, gathered[0], gathered[1], gathered[4])
    )
    after, unused = lax.scan(
        backward_step, blank, (group_ids, gathered[2], gathered[3], gathered[4]), reverse=True
    )
    open_front = first_pick * continued[:, None]
    seg_total = (
        seg_sums
        + open_front[:, :, None] * before[0][:, None, :]
        + last_pick[:, :, None] * after[0][:, None, :]
    )
    weight_total = seg_weights + open_front * before[1][:, None] + last_pick * after[1][:, None]
    leaf_sums = jnp.einsum("tgl,tgn->ltn", member, seg_total, precision=highest)
    leaf_weights = jnp.einsum("tgl,tg->lt", member, weight_total, precision=highest)
    average = leaf_sums / leaf_weights[:, :, None]
    new_dual = dual + penalty * (state - average)
    return (state, average, new_dual)


def solution(mesh):
    return jax.shard_map(
        local,
        mesh=mesh,
        in_specs=(
            P("scen", None, "feeder"),
            P("scen", None, "feeder"),
            P("scen", None, "feeder"),
            P("scen", None),
            P("scen"),
            P("feeder", None),
            P("feeder"),
            P("feeder", None, None),
            P(None, "scen"),
        ),
        out_specs=(P("scen", None, "feeder"), P("scen", None, "feeder"), P("scen", None, "feeder")),
        check_vma=False,
    )
```

profile of v0, /device:TPU:32, one launch (start us, length us, event | category | flops | bytes accessed | tf_op | source)
XLA Modules:
  0.0 681.2 jit_solution(15530600553333728089)
XLA Ops:
  0.6 0.7 convert_bitcast_fusion
  1.4 0.6 broadcast_in_dim.11
  2.1 0.9 copy-done
  3.0 0.4 fusion.100
  3.9 68.3 %psum.56 = f32[16,24]{1,0:T(8,128)S(1)} all-reduce(f32[16,24]{1,0:T(8,128)S(1)} %convert_reduce_fusion), channel_id=1, replica_groups=mesh['feeder'=32,'scen'=16] {'feeder'}, use_global_device_ids=true, to_apply=%region_1.0 | all-reduce | flops 384 | bytes 3072 | tf_op jit(solution)/shard_map/psum | solution.py:38
  72.2 1.4 fusion.74
  73.6 63.7 %psum.57 = f32[16,24]{1,0:T(8,128)S(1)} all-reduce(f32[16,24]{1,0:T(8,128)S(1)} %get-tuple-element.314), channel_id=1, replica_groups=mesh['feeder'=32,'scen'=16] {'feeder'}, use_global_device_ids=true, to_apply=%region_3.4 | all-reduce | flops 384 | bytes 3072 | tf_op jit(solution)/shard_map/psum | solution.py:38
  137.4 0.9 fusion.93
  138.2 63.7 %psum.58 = f32[16,24]{1,0:T(8,128)S(1)} all-reduce(f32[16,24]{1,0:T(8,128)S(1)} %get-tuple-element.320), channel_id=1, replica_groups=mesh['feeder'=32,'scen'=16] {'feeder'}, use_global_device_ids=true, to_apply=%region_5.6 | all-reduce | flops 384 | bytes 3072 | tf_op jit(solution)/shard_map/psum | solution.py:38
  201.9 0.6 fusion.94
  202.5 63.7 %psum.59 = f32[16,24]{1,0:T(8,128)S(1)} all-reduce(f32[16,24]{1,0:T(8,128)S(1)} %get-tuple-element.322), channel_id=1, replica_groups=mesh['feeder'=32,'scen'=16] {'feeder'}, use_global_device_ids=true, to_apply=%region_7.8 | all-reduce | flops 384 | bytes 3072 | tf_op jit(solution)/shard_map/psum | solution.py:38
  266.2 0.6 fusion.95
  266.8 63.7 %psum.60 = f32[16,24]{1,0:T(8,128)S(1)} all-reduce(f32[16,24]{1,0:T(8,128)S(1)} %get-tuple-element.324), channel_id=1, replica_groups=mesh['feeder'=32,'scen'=16] {'feeder'}, use_global_device_ids=true, to_apply=%region_9.10 | all-reduce | flops 384 | bytes 3072 | tf_op jit(solution)/shard_map/psum | solution.py:38
  330.5 0.6 fusion.96
  331.1 63.7 %psum.61 = f32[16,24]{1,0:T(8,128)S(1)} all-reduce(f32[16,24]{1,0:T(8,128)S(1)} %get-tuple-element.326), channel_id=1, replica_groups=mesh['feeder'=32,'scen'=16] {'feeder'}, use_global_device_ids=true, to_apply=%region_11.12 | all-reduce | flops 384 | bytes 3072 | tf_op jit(solution)/shard_map/psum | solution.py:38
  394.8 1.4 fusion.97
  396.1 63.7 %psum.62 = f32[16,24]{1,0:T(8,128)S(1)} all-reduce(f32[16,24]{1,0:T(8,128)S(1)} %get-tuple-element.328), channel_id=1, replica_groups=mesh['feeder'=32,'scen'=16] {'feeder'}, use_global_device_ids=true, to_apply=%region_13.14 | all-reduce | flops 384 | bytes 3072 | tf_op jit(solution)/shard_map/psum | solution.py:38
  459.8 2.0 fusion.98
  461.8 63.7 %psum.63 = f32[16,24]{1,0:T(8,128)S(1)} all-reduce(f32[16,24]{1,0:T(8,128)S(1)} %get-tuple-element.330), channel_id=1, replica_groups=mesh['feeder'=32,'scen'=16] {'feeder'}, use_global_device_ids=true, to_apply=%region_15.16 | all-reduce | flops 384 | bytes 3072 | tf_op jit(solution)/shard_map/psum | solution.py:38
  525.5 0.6 copy-done.8
  526.2 1.4 broadcast_multiply_fusion
  527.5 0.7 copy-done.6
  528.3 1.0 fusion.48
  529.5 0.4 fusion.99
  529.9 37.7 %all-gather = f32[384,512]{1,0:T(8,128)S(1)} all-gather(f32[24,512]{1,0:T(8,128)S(1)} %bitcast.122), channel_id=2, replica_groups=mesh['feeder'=32,'scen'=16] {'scen'}, dimensions={0}, use_global_device_ids=true | all-gather | bytes 835584 | tf_op jit(solution)/shard_map/all_gather | solution.py:59
  568.0 1.3 dynamic-slice
  570.3 30.1 %all-reduce.3 = (f32[384]{0:T(512)S(1)}, f32[384]{0:T(512)S(1)}, f32[384]{0:T(512)S(1)}) all-reduce(f32[384]{0:T(512)S(1)} %fusion.86, f32[384]{0:T(512)S(1)} %fusion.84, f32[384]{0:T(512)S(1)} %dynamic-update-slice.1), channel_id=3, replica_groups=mesh['feeder'=32,'scen'=16] {'scen'}, use_global_device_ids=true, to_apply=%add | all-reduce | flops 1152 | bytes 9216
  600.6 23.5 %while.30 = (s32[]{:T(128)}, f32[24,512]{1,0:T(8,128)S(1)}, f32[24]{0:T(128)S(1)}, s32[16]{0:T(128)S(1)}, s32[]{:T(128)}, /*index=5*/f32[16,24,512]{2,1,0:T(8,12...) while((s32[]{:T(128)}, f32[24,512]{1,0:T(8,128)S(1)}, ...), condition=%wide.region_18.19_spmd.clone, body=%wide.region_17.18_spmd.clone.sunk | while | flops 49252 | bytes 148175 | solution.py:87
  600.6 0.7 dynamic_slice.91
  602.1 0.7 dynamic_slice.91
  603.5 0.7 dynamic_slice.91
  605.0 0.7 dynamic_slice.91
  606.5 0.7 dynamic_slice.91
  607.9 0.7 dynamic_slice.91
  609.4 0.7 dynamic_slice.91
  610.9 0.7 dynamic_slice.91
  612.3 0.7 dynamic_slice.91
  613.8 0.7 dynamic_slice.91
  615.3 0.7 dynamic_slice.91
  616.7 0.7 dynamic_slice.91
  618.2 0.7 dynamic_slice.91
  619.7 0.7 dynamic_slice.91
  621.1 0.7 dynamic_slice.91
  622.6 0.7 dynamic_slice.91
  624.2 30.1 %all_gather.18 = f32[16,24,512]{2,1,0:T(8,128)S(1)} all-gather(f32[1,24,512]{2,1,0:T(8,128)S(1)} %copy.24), channel_id=1, replica_groups=mesh['feeder'=32,'scen'=16] {'scen'}, dimensions={0}, use_global_device_ids=true | all-gather | bytes 835584 | tf_op jit(solution)/shard_map/all_gather | solution.py:61
  654.4 23.5 %while.31 = (s32[]{:T(128)}, f32[24,512]{1,0:T(8,128)S(1)}, f32[24]{0:T(128)S(1)}, s32[16]{0:T(128)S(1)}, s32[]{:T(128)}, /*index=5*/f32[16,24,512]{2,1,0:T(8,12...) while((s32[]{:T(128)}, f32[24,512]{1,0:T(8,128)S(1)}, ...), condition=%wide.region_20.21_spmd.clone, body=%wide.region_19.20_spmd.clone.sunk | while | flops 49253 | bytes 148195 | solution.py:90
  654.4 0.7 dynamic_slice.94
  655.9 0.7 dynamic_slice.94
  657.4 0.7 dynamic_slice.94
  658.9 0.7 dynamic_slice.94
  660.3 0.7 dynamic_slice.94
  661.8 0.7 dynamic_slice.94
  663.3 0.7 dynamic_slice.94
  664.7 0.7 dynamic_slice.94
  666.2 0.7 dynamic_slice.94
  667.7 0.7 dynamic_slice.94
  669.1 0.7 dynamic_slice.94
  670.6 0.7 dynamic_slice.94
  672.1 0.7 dynamic_slice.94
  673.5 0.7 dynamic_slice.94
  675.0 0.7 dynamic_slice.94
  676.5 0.7 dynamic_slice.94
  678.2 0.7 fusion.50
  679.5 1.7 subtract_add_fusion
  (125 shorter events, 6.0 us)
Async XLA Ops:
  0.6 1.4 copy-start.4
  2.0 1.0 copy-start
  3.0 0.7 copy-start.7
  3.0 69.2 %copy-start.2 = (f32[16,24,512]{2,1,0:T(8,128)S(1)}, f32[16,24,512]{2,1,0:T(8,128)}, u32[]{:S(2)}) copy-start(f32[16,24,512]{2,1,0:T(8,128)} %param.15) | copy-start | bytes 2359300
  3.8 68.4 %copy-start.5 = (f32[16,24]{1,0:T(8,128)S(1)}, f32[16,24]{1,0:T(8,128)}, u32[]{:S(2)}) copy-start(f32[16,24]{1,0:T(8,128)} %param.16) | copy-start | bytes 4612
  525.5 0.7 copy-start.8
  527.5 0.7 copy-start.6
  678.2 1.1 copy-start.1
  678.2 1.4 copy-start.3
where the time goes:
time: 682 us; the launch traced here: 681 us
  blocking collectives  612 us (90%)
  local copies, waits for them, and re-layouts  27 us (4%)
  loops' own time  22.6 us (3%)
  matrix products  10.1 us (1%)
  other arithmetic  7.87 us (1%)
    psum x8, blocking collectives, local(): head = lax.psum(jnp.sum(state, axis=2), 'feeder') / total_nodes  514 us
    all_gather x1, blocking collectives, local(): lax.all_gather(tail_sum[None], 'scen', axis=0, tiled=True)  37.7 us
    all_gather x1, blocking collectives, local(): lax.all_gather(head_sum[None], 'scen', axis=0, tiled=True)  30.1 us
    unnamed x1, blocking collectives  30.1 us
    dynamic_slice x32, local copies, waits for them, and re-layouts, local(): lax.scan(forward_step, blank, (group_ids, gathered[0], gathered[1], gathe...  21.2 us

commit v1 on v0

--- a/solution.py
+++ b/solution.py
@@ -58,7 +58,10 @@
     gathered = (
         lax.all_gather(tail_sum[None], "scen", axis=0, tiled=True),
         lax.all_gather(tail_weight[None], "scen", axis=0, tiled=True),
-        lax.all_gather(head_sum[None], "scen", axis=0, tiled=True),
+        jnp.concatenate(
+            lax.all_to_all(jnp.stack([head_sum[None]] * lax.axis_size("scen")), "scen", 0, 0),
+            axis=0,
+        ),
         lax.all_gather(head_weight[None], "scen", axis=0, tiled=True),
         lax.all_gather(spanning[None], "scen", axis=0, tiled=True),
     )

time: 682 us -> 704 us (1.032)
  starting transfers between devices: 0 us -> 15.1 us
  other arithmetic: 7.87 us -> 22.9 us
    all_gather x1 -> x0, blocking collectives: 30.1 us -> none  [local(): lax.all_gather(head_sum[None], 'scen', axis=0, tiled=True)]
    all_gather x1, blocking collectives: 37.7 us -> 64.3 us  [local(): lax.all_gather(tail_sum[None], 'scen', axis=0, tiled=True)]
    all_to_all x0 -> x1, starting transfers between devices: none -> 15.1 us  [local(): lax.all_to_all(jnp.stack([head_sum[None]] * lax.axis_size('scen')), 'scen...]
    select_n x32, other arithmetic: 1.58 us -> 14.4 us  [forward_step(): jnp.where(keep, new_val, old_val)]
  transfers between devices with their start and end apart: 0 -> 1, of which waited for: 0 -> 0; matrix products, arithmetic and copies ran while one was open for 0% -> 4% of each run, Pallas kernels for 0% -> 0%
where the time goes in v1:
time: 704 us; the launch traced here: 702 us
  blocking collectives  608 us (86%)
  local copies, waits for them, and re-layouts  26.5 us (4%)
  other arithmetic  22.9 us (3%)
  loops' own time  20.9 us (3%)
  starting transfers between devices  15.1 us (2%)
    psum x8, blocking collectives, local(): head = lax.psum(jnp.sum(state, axis=2), 'feeder') / total_nodes  514 us
    all_gather x1, blocking collectives, local(): lax.all_gather(tail_sum[None], 'scen', axis=0, tiled=True)  64.3 us
    unnamed x1, blocking collectives  29.3 us
    dynamic_slice x32, local copies, waits for them, and re-layouts, local(): lax.scan(forward_step, blank, (group_ids, gathered[0], gathered[1], gathe...  19.7 us
    all_to_all x1, starting transfers between devices, local(): lax.all_to_all(jnp.stack([head_sum[None]] * lax.axis_size('scen')), 'scen...  15.1 us
    select_n x32, other arithmetic, forward_step(): jnp.where(keep, new_val, old_val)  14.4 us
  transfers between devices with their start and end apart: 1, of which 0 were waited for; matrix products, arithmetic and copies ran while one was open for 4% of the time, Pallas kernels for 0%

profile of v1, /device:TPU:32, one launch (start us, length us, event | category | flops | bytes accessed | tf_op | source)
XLA Modules:
  0.0 702.0 jit_solution(9320012420796091418)
XLA Ops:
  0.6 0.7 subtract_maximum_fusion
  1.4 0.7 fusion.81
  2.1 1.2 convert_reduce_fusion
  3.3 68.3 %psum.56 = f32[16,24]{1,0:T(8,128)S(1)} all-reduce(f32[16,24]{1,0:T(8,128)S(1)} %convert_reduce_fusion), channel_id=1, replica_groups=mesh['feeder'=32,'scen'=16] {'feeder'}, use_global_device_ids=true, to_apply=%region_1.0 | all-reduce | flops 384 | bytes 3072 | tf_op jit(solution)/shard_map/psum | solution.py:38
  71.7 0.6 broadcast_in_dim.11
  72.4 0.9 copy-done
  75.0 63.7 %psum.57 = f32[16,24]{1,0:T(8,128)S(1)} all-reduce(f32[16,24]{1,0:T(8,128)S(1)} %get-tuple-element.306), channel_id=1, replica_groups=mesh['feeder'=32,'scen'=16] {'feeder'}, use_global_device_ids=true, to_apply=%region_3.4 | all-reduce | flops 384 | bytes 3072 | tf_op jit(solution)/shard_map/psum | solution.py:38
  138.7 0.9 fusion.92
  139.5 63.7 %psum.58 = f32[16,24]{1,0:T(8,128)S(1)} all-reduce(f32[16,24]{1,0:T(8,128)S(1)} %get-tuple-element.312), channel_id=1, replica_groups=mesh['feeder'=32,'scen'=16] {'feeder'}, use_global_device_ids=true, to_apply=%region_5.6 | all-reduce | flops 384 | bytes 3072 | tf_op jit(solution)/shard_map/psum | solution.py:38
  203.8 63.7 %psum.59 = f32[16,24]{1,0:T(8,128)S(1)} all-reduce(f32[16,24]{1,0:T(8,128)S(1)} %get-tuple-element.314), channel_id=1, replica_groups=mesh['feeder'=32,'scen'=16] {'feeder'}, use_global_device_ids=true, to_apply=%region_7.8 | all-reduce | flops 384 | bytes 3072 | tf_op jit(solution)/shard_map/psum | solution.py:38
  268.1 63.7 %psum.60 = f32[16,24]{1,0:T(8,128)S(1)} all-reduce(f32[16,24]{1,0:T(8,128)S(1)} %get-tuple-element.316), channel_id=1, replica_groups=mesh['feeder'=32,'scen'=16] {'feeder'}, use_global_device_ids=true, to_apply=%region_9.10 | all-reduce | flops 384 | bytes 3072 | tf_op jit(solution)/shard_map/psum | solution.py:38
  332.4 63.7 %psum.61 = f32[16,24]{1,0:T(8,128)S(1)} all-reduce(f32[16,24]{1,0:T(8,128)S(1)} %get-tuple-element.318), channel_id=1, replica_groups=mesh['feeder'=32,'scen'=16] {'feeder'}, use_global_device_ids=true, to_apply=%region_11.12 | all-reduce | flops 384 | bytes 3072 | tf_op jit(solution)/shard_map/psum | solution.py:38
  396.7 63.7 %psum.62 = f32[16,24]{1,0:T(8,128)S(1)} all-reduce(f32[16,24]{1,0:T(8,128)S(1)} %get-tuple-element.320), channel_id=1, replica_groups=mesh['feeder'=32,'scen'=16] {'feeder'}, use_global_device_ids=true, to_apply=%region_13.14 | all-reduce | flops 384 | bytes 3072 | tf_op jit(solution)/shard_map/psum | solution.py:38
  461.0 63.7 %psum.63 = f32[16,24]{1,0:T(8,128)S(1)} all-reduce(f32[16,24]{1,0:T(8,128)S(1)} %get-tuple-element.322), channel_id=1, replica_groups=mesh['feeder'=32,'scen'=16] {'feeder'}, use_global_device_ids=true, to_apply=%region_15.16 | all-reduce | flops 384 | bytes 3072 | tf_op jit(solution)/shard_map/psum | solution.py:38
  524.8 0.7 copy-done.9
  525.9 1.0 fusion.48
  527.1 1.0 stack.3
  528.1 15.1 %all-to-all-start = ((f32[16,1,24,512]{3,2,1,0:T(8,128)}), f32[16,1,24,512]{3,2,1,0:T(8,128)S(1)}, u32[]{:S(2)}, u32[]{:S(2)}) async-start(f32[16,1,24,512]{3,2,1,0:T(8,128)} %stack.3), calls=%async_computation | async-start | bytes 1572864 | tf_op jit(solution)/shard_map/all_to_all | solution.py:62
  544.0 64.3 %all-gather = f32[384,512]{1,0:T(8,128)} all-gather(f32[24,512]{1,0:T(8,128)S(1)} %bitcast.122), channel_id=2, replica_groups=mesh['feeder'=32,'scen'=16] {'scen'}, dimensions={0}, use_global_device_ids=true | all-gather | bytes 835584 | tf_op jit(solution)/shard_map/all_gather | solution.py:59
  608.5 1.3 dynamic-slice
  610.5 0.8 fusion.85
  611.4 0.8 fusion.83
  612.2 29.3 %all-reduce.3 = (f32[384]{0:T(512)S(1)}, f32[384]{0:T(512)S(1)}, f32[384]{0:T(512)S(1)}) all-reduce(f32[384]{0:T(512)S(1)} %fusion.85, f32[384]{0:T(512)S(1)} %fusion.83, f32[384]{0:T(512)S(1)} %dynamic-update-slice.1), channel_id=3, replica_groups=mesh['feeder'=32,'scen'=16] {'scen'}, use_global_device_ids=true, to_apply=%add | all-reduce | flops 1152 | bytes 9216
  641.7 35.1 %while.30 = (s32[]{:T(128)}, f32[24,512]{1,0:T(8,128)S(1)}, f32[24]{0:T(128)S(1)}, s32[16]{0:T(128)S(1)}, s32[]{:T(128)}, /*index=5*/f32[16,24,512]{2,1,0:T(8,12...) while((s32[]{:T(128)}, f32[24,512]{1,0:T(8,128)S(1)}, ...), condition=%wide.region_18.19_spmd.clone, body=%wide.region_17.18_spmd.clone.sunk | while | flops 49252 | bytes 148175 | solution.py:90
  641.7 0.7 dynamic_slice.91
  643.1 0.9 fusion.106
  643.9 0.6 dynamic_slice.91
  645.3 0.9 fusion.106
  646.1 0.6 dynamic_slice.91
  647.4 0.9 fusion.106
  648.3 0.6 dynamic_slice.91
  649.6 0.9 fusion.106
  650.5 0.6 dynamic_slice.91
  651.8 0.9 fusion.106
  652.7 0.6 dynamic_slice.91
  654.0 0.9 fusion.106
  654.9 0.6 dynamic_slice.91
  656.2 0.9 fusion.106
  657.1 0.6 dynamic_slice.91
  658.4 0.9 fusion.106
  659.3 0.6 dynamic_slice.91
  660.6 0.9 fusion.106
  661.5 0.6 dynamic_slice.91
  662.8 0.9 fusion.106
  663.7 0.6 dynamic_slice.91
  665.0 0.9 fusion.106
  665.9 0.6 dynamic_slice.91
  667.2 0.9 fusion.106
  668.0 0.6 dynamic_slice.91
  669.4 0.9 fusion.106
  670.2 0.6 dynamic_slice.91
  671.6 0.9 fusion.106
  672.4 0.6 dynamic_slice.91
  673.7 0.9 fusion.106
  674.6 0.6 dynamic_slice.91
  675.9 0.9 fusion.106
  677.0 21.5 %while.31 = (s32[]{:T(128)}, f32[24,512]{1,0:T(8,128)S(1)}, f32[24]{0:T(128)S(1)}, s32[16]{0:T(128)S(1)}, s32[]{:T(128)}, /*index=5*/f32[16,24,512]{2,1,0:T(8,12...) while((s32[]{:T(128)}, f32[24,512]{1,0:T(8,128)S(1)}, ...), condition=%wide.region_20.21_spmd.clone, body=%wide.region_19.20_spmd.clone.sunk | while | flops 49253 | bytes 148195 | solution.py:93
  677.0 0.6 dynamic_slice.94
  678.4 0.6 dynamic_slice.94
  679.7 0.6 dynamic_slice.94
  681.0 0.6 dynamic_slice.94
  686.4 0.6 dynamic_slice.94
  699.0 0.7 fusion.50
  700.2 1.8 subtract_add_fusion
  (129 shorter events, 16.1 us)
Async XLA Ops:
  0.6 1.4 copy-start.7
  1.4 0.7 copy-start.8
  2.1 70.2 %copy-start.4 = (bf16[512,512]{1,0:T(8,128)(2,1)S(1)}, bf16[512,512]{1,0:T(8,128)(2,1)}, u32[]{:S(2)}) copy-start(bf16[512,512]{1,0:T(8,128)(2,1)} %param.18) | copy-start | bytes 1572868
  72.3 1.0 copy-start
  73.3 0.7 copy-start.5
  73.3 1.1 copy-start.2
  73.3 1.2 copy-start.6
  524.8 0.7 copy-start.9
  525.9 173.8 %copy-start.1 = (f32[16,24,512]{2,1,0:T(8,128)}, f32[16,24,512]{2,1,0:T(8,128)S(1)}, u32[]{:S(2)}) copy-start(f32[16,24,512]{2,1,0:T(8,128)S(1)} %get-tuple-element.325) | copy-start | bytes 2359300
  528.1 148.9 %all-to-all-start = ((f32[16,1,24,512]{3,2,1,0:T(8,128)}), f32[16,1,24,512]{3,2,1,0:T(8,128)S(1)}, u32[]{:S(2)}, u32[]{:S(2)}) async-start(f32[16,1,24,512]{3,2,1,0:T(8,128)} %stack.3), calls=%async_computation | async-start | bytes 1572864 | tf_op jit(solution)/shard_map/all_to_all | solution.py:62
  699.0 1.1 copy-start.3
